TPU v7x, 128 devices: a whole 4x4x4 slice. The times are simulated.
128 devices in a mesh: exp: 32 (over z, x_lo, y), row: 4 (over x_hi, core).
Axes of the slice: x: 4 (x_hi: 2, x_lo: 2; x = x_hi * 2 + x_lo), y: 4, z: 4, core: 2. Of those that a mesh axis runs over, the one named last changes fastest.
Arguments:
- latent: bfloat16 [4, 1024, 1024], P(None, 'row', 'exp'), may hold values from -6 to 6
- row_taps: bfloat16 [16, 21], replicated, may hold values from -1.25 to 1.25
- column_taps: bfloat16 [16, 21], replicated, may hold values from -1.25 to 1.25
- coefficients: bfloat16 [32, 16, 1024, 1024], P('exp', None, 'row'), may hold values from -1.5 to 1.5
- observed: bfloat16 [32, 1024, 1024], P('exp', 'row'), may hold values from -6 to 6
- cell_of: int32 [32, 1], replicated, may hold values from 0 to 3
- valid_rows: int32 [32, 1024], P('exp', 'row'), may hold values 0 or 1
Outputs:
- gradient: float32 [4, 1024, 1024], P(None, 'row', 'exp')
- residuals: float32 [32, 1024, 1024], P('exp', 'row')
Inputs may be any that keep to these rules, and one draw needn't show every extreme that they name: `cell_of`: every sky cell is covered by at least one exposure.
All inputs are finite; a program needn't handle non-finite values. No bound on the sum of `valid_rows` on one device may be relied on, other than what follows from the above.
Results may differ from a plain program's by a relative error of at most 0.0023.
Values may be sent and summed in bfloat16 or wider, within the bound.
No kernel may reach another device: no remote copies, remote signals or barrier semaphores. Data moves between devices by JAX's collectives and lax.ppermute only.
A program may use at most 128 MiB of HBM per device.

v0:
```python
import jax
import jax.numpy as jnp
from jax import lax
from jax.sharding import PartitionSpec as P


def padded_2(cells, sides, width):
    for axis, dim in sides:
        count = lax.axis_size(axis)
        ends = count - 1
        head = lax.slice_in_dim(cells, 0, width, axis=dim)
        tail = lax.slice_in_dim(cells, cells.shape[dim] - width, cells.shape[dim], axis=dim)
        cells = jnp.concatenate(
            [
                lax.ppermute(tail, axis, [(i, (i + 1) % count) for i in range(ends)]),
                cells,
                lax.ppermute(head, axis, [((i + 1) % count, i) for i in range(ends)]),
            ],
            axis=dim,
        )
    return cells


def from_behind(block, axis, distance):
    devices = range(lax.axis_size(axis))
    route = [(i - distance, i) for i in devices if i - distance in devices]
    return lax.ppermute(block, axis, route)


def bands(kernel_taps, adjoint):
    tap_count = kernel_taps.shape[1]
    halfwidth = tap_count // 2
    inputs_at = lax.broadcasted_iota(jnp.int32, (384, 128), 0)
    outputs_at = lax.broadcasted_iota(jnp.int32, (384, 128), 1)
    if adjoint:
        offset = outputs_at - inputs_at + 128 + halfwidth
    else:
        offset = inputs_at - 128 - outputs_at + halfwidth
    onehot = (offset[:, :, None] == jnp.arange(tap_count)[None, None, :]).astype(jnp.float32)
    return jnp.einsum("kt,pqt->kpq", kernel_taps.astype(jnp.float32), onehot).astype(jnp.bfloat16)


def column_matrix(kernel_taps, strip_rows):
    tap_count = kernel_taps.shape[1]
    halfwidth = tap_count // 2
    outputs_at = lax.broadcasted_iota(jnp.int32, (strip_rows, strip_rows + 2 * halfwidth), 0)
    inputs_at = lax.broadcasted_iota(jnp.int32, (strip_rows, strip_rows + 2 * halfwidth), 1)
    offset = inputs_at - outputs_at
    onehot = (offset[:, :, None] == jnp.arange(tap_count)[None, None, :]).astype(jnp.float32)
    return jnp.einsum("kt,yit->kyi", kernel_taps.astype(jnp.float32), onehot).astype(jnp.bfloat16)


def stacked_blocks(source):
    length = source.shape[-1]
    nblocks = length // 128
    padding = [(0, 0)] * (source.ndim - 1) + [(128, 128)]
    padded = jnp.pad(source, padding)
    blocked = padded.reshape(source.shape[:-1] + (nblocks + 2, 128))
    return jnp.concatenate(
        [blocked[..., :-2, :], blocked[..., 1:-1, :], blocked[..., 2:, :]], axis=-1
    )


def body(latent, row_taps, column_taps, coefficients, observed, cell_of, valid_rows):
    tap_count = row_taps.shape[1]
    halfwidth = tap_count // 2
    kernel_count = row_taps.shape[0]
    strip_rows = observed.shape[1]
    cell_width = observed.shape[2]
    ncells = latent.shape[0]
    position = lax.axis_index("exp")
    cell_list = cell_of[:, 0]
    own_cell = lax.dynamic_index_in_dim(cell_list, position, 0, keepdims=False)
    all_cells = lax.all_gather(latent, "exp", axis=2, tiled=True)
    cell_strip = lax.dynamic_index_in_dim(all_cells, own_cell, 0, keepdims=False)
    extended = padded_2(cell_strip, (("row", 0),), halfwidth)
    rowblur = jnp.einsum(
        "rbp,kpq->krbq",
        stacked_blocks(extended),
        bands(row_taps, False),
        preferred_element_type=jnp.float32,
    )
    rowblur = rowblur.reshape(kernel_count, strip_rows + 2 * halfwidth, cell_width).astype(
        jnp.bfloat16
    )
    matrix = column_matrix(column_taps, strip_rows)
    vertical = jnp.einsum("kyi,kix->kyx", matrix, rowblur, preferred_element_type=jnp.float32)
    coeffs = coefficients[0].astype(jnp.float32)
    predicted = jnp.sum(coeffs * vertical, axis=0)
    row_mask = valid_rows[0].astype(jnp.float32)[:, None]
    residual = row_mask * (predicted - observed[0].astype(jnp.float32))
    weighted = (coeffs * residual[None]).astype(jnp.bfloat16)
    colback_ext = jnp.einsum("kyi,kyx->kix", matrix, weighted, preferred_element_type=jnp.float32)
    upper_rim = colback_ext[:, :halfwidth]
    lower_rim = colback_ext[:, strip_rows + halfwidth :]
    from_below = from_behind(upper_rim.astype(jnp.bfloat16), "row", -1).astype(upper_rim.dtype)
    from_above = from_behind(lower_rim.astype(jnp.bfloat16), "row", 1).astype(lower_rim.dtype)
    middle = colback_ext[:, halfwidth : strip_rows + halfwidth]
    middle = middle.at[:, :halfwidth].add(from_above)
    middle = middle.at[:, strip_rows - halfwidth :].add(from_below)
    colback = middle.astype(jnp.bfloat16)
    own_term = jnp.einsum(
        "krbp,kpq->rbq",
        stacked_blocks(colback),
        bands(row_taps, True),
        preferred_element_type=jnp.float32,
    ).reshape(strip_rows, cell_width)
    selector = (jnp.arange(ncells) == own_cell).astype(jnp.float32)
    gradient = lax.psum_scatter(
        selector[:, None, None] * own_term[None], "exp", scatter_dimension=2, tiled=True
    )
    return (gradient, residual[None])


def solution(mesh):
    placed = (
        P(None, "row", "exp"),
        P(),
        P(),
        P("exp", None, "row", None),
        P("exp", "row", None),
        P(),
        P("exp", "row"),
    )
    return jax.shard_map(
        body,
        mesh=mesh,
        in_specs=placed,
        out_specs=(P(None, "row", "exp"), P("exp", "row", None)),
        check_vma=False,
    )
```

profile of v0, /device:TPU:4, one launch (start us, length us, event | category | flops | bytes accessed | tf_op | source)
XLA Modules:
  0.0 556.6 jit_solution(14296747167301705185)
XLA Ops:
  7.2 1.5 copy.41
  11.9 2.3 fusion.28
  14.2 2.2 convert_bitcast_fusion.1
  16.4 148.6 %all-gather.2.cloned.1.call-done = bf16[4,256,1024]{1,0,2:T(4,128)(2,1)} async-done(((bf16[4,256,32]{1,0,2:T(4,128)(2,1)}), bf16[4,256,1024]{1,0,2:T(4,128)(2,1)}) %all-gather.2.cloned.1.call-update) | async-done | bytes 2097168 | tf_op jit(solution)/shard_map/all_gather | solution.py:74
  165.0 2.7 constant_dynamic-slice_fusion
  167.7 2.3 copy.62
  170.7 1.9 collective-permute-start
  172.7 5.3 collective-permute-start.1
  179.4 2.0 fusion.36
  184.4 7.2 %convert_bitcast_fusion = bf16[16,276,8,128]{3,1,2,0:T(8,128)(2,1)} fusion(bf16[276,8,128]{2,0,1:T(8,128)(2,1)S(1)} %copy.65, bf16[276,8,128]{2,0,1:T(8,128)(2,1)S(1)} %copy.64, bf16[276,8,128]{2,0,1:T(8,128)(2,1)S(1)} %copy.63, bf16[16,384,128,1]{2,0,1,3:T(8,128)(2,1)S(1)} %copy-done.3), kind=kOutput, calls=%fused_computation.10 | convolution fusion | flops 3482492928 | bytes 12312576 | tf_op jit(solution)/shard_map/rbp,kpq->krbq/dot_general | solution.py:77
  191.6 8.3 %copy.60 = bf16[16,276,8,128]{3,2,1,0:T(8,128)(2,1)} copy(bf16[16,276,8,128]{3,1,2,0:T(8,128)(2,1)} %convert_bitcast_fusion) | data formatting | bytes 18087936 | tf_op jit(solution)/shard_map/convert_element_type | solution.py:83
  199.9 14.0 %reshape.143 = bf16[16,276,1024]{2,1,0:T(8,128)(2,1)} reshape(bf16[16,276,8,128]{3,2,1,0:T(8,128)(2,1)} %copy.60) | data formatting | bytes 18087936 | tf_op jit(solution)/shard_map/convert_element_type | solution.py:83
  213.8 13.0 %fusion.6 = f32[256,1024]{1,0:T(8,128)S(1)} fusion(bf16[16,276,1024]{2,1,0:T(8,128)(2,1)} %reshape.143, bf16[1,16,256,1024]{3,2,1,0:T(8,128)(2,1)} %param.14, bf16[16,256,276]{1,0,2:T(8,128)(2,1)S(1)} %convert_bitcast_fusion.1), kind=kOutput, calls=%fused_computation.8 | convolution fusion | flops 2327576576 | bytes 20742144 | tf_op jit(solution)/shard_map/kyi,kix->kyx/dot_general | solution.py:87
  227.0 17.7 %fusion.45 = (bf16[16,276,1024]{2,1,0:T(8,128)(2,1)}, f32[16,276,1024]{2,1,0:T(8,128)}) fusion(bf16[1,16,256,1024]{3,2,1,0:T(8,128)(2,1)} %param.14, f32[256,1024]{1,0:T(8,128)S(1)} %bitcast.54, bf16[16,256,276]{1,0,2:T(8,128)(2,1)S(1)} %convert_bitcast_fusion.1), kind=kOutput, calls=%fused_computation.67 | convolution fusion | flops 2332360704 | bytes 38830080 | tf_op jit(solution)/shard_map/kyi,kyx->kix/dot_general | solution.py:93
  244.7 2.4 fusion.43
  247.1 1.9 collective-permute-start.2
  250.1 5.2 collective-permute-start.3
  257.1 12.6 %slice.110 = f32[16,256,1024]{2,1,0:T(8,128)} slice(f32[16,276,1024]{2,1,0:T(8,128)} %get-tuple-element.37), slice={[0:16], [10:266], [0:1024]} | slice | bytes 33554432 | tf_op jit(solution)/shard_map/slice | solution.py:98
  269.7 1.7 slice_add_fusion.1
  271.4 5.8 %scatter-add.6 = f32[16,256,1024]{2,1,0:T(8,128)} dynamic-update-slice(f32[16,256,1024]{2,1,0:T(8,128)} %slice.110, f32[16,10,1024]{2,1,0:T(8,128)S(1)} %slice_add_fusion.1, s32[]{:T(128)} %constant.75.clone.1, s32[]{:T(128)} %constant.75.clone.1, s32[]{:T(128)} %constant.75.clone.1) | dynamic-update-slice | bytes 1310724 | tf_op jit(solution)/shard_map/scatter-add | solution.py:99
  277.3 1.5 slice_add_fusion
  278.8 5.1 scatter-add.9
  283.9 9.1 %convert_element_type.94 = bf16[16,256,1024]{2,1,0:T(8,128)(2,1)} convert(f32[16,256,1024]{2,1,0:T(8,128)} %scatter-add.9) | non-fusion elementwise | flops 4194304 | bytes 25165824 | tf_op jit(solution)/shard_map/convert_element_type | solution.py:101
  293.0 12.3 %copy.69 = bf16[16,256,1024]{1,2,0:T(8,128)(2,1)} copy(bf16[16,256,1024]{2,1,0:T(8,128)(2,1)} %convert_element_type.94) | data formatting | bytes 16777216
  305.3 8.4 %pad.13.clone = bf16[16,256,1280]{1,2,0:T(8,128)(2,1)} pad(bf16[16,256,1024]{1,2,0:T(8,128)(2,1)} %copy.69, bf16[]{:T(256)} %constant.80.clone.1), padding=0_0x0_0x128_128 | pad | bytes 18874370 | tf_op jit(solution)/shard_map/jit(_pad)/pad | solution.py:57
  313.7 16.7 %fusion.42 = (bf16[16,256,8,128]{1,3,2,0:T(8,128)(2,1)}, bf16[16,256,8,128]{1,3,2,0:T(8,128)(2,1)}, bf16[16,256,8,128]{1,3,2,0:T(8,128)(2,1)}) fusion(bf16[16,256,10,128]{1,3,2,0:T(8,128)(2,1)} %bitcast.53), kind=kLoop, calls=%fused_computation.64 | loop fusion | bytes 50331648 | tf_op jit(solution)/shard_map/slice | solution.py:60
  330.4 11.4 %copy.66 = bf16[16,256,8,128]{3,1,0,2:T(8,128)(2,1)} copy(bf16[16,256,8,128]{1,3,2,0:T(8,128)(2,1)} %get-tuple-element.26) | data formatting | bytes 16777216
  341.8 11.4 %copy.67 = bf16[16,256,8,128]{3,1,0,2:T(8,128)(2,1)} copy(bf16[16,256,8,128]{1,3,2,0:T(8,128)(2,1)} %get-tuple-element.27) | data formatting | bytes 16777216
  353.2 11.4 %copy.68 = bf16[16,256,8,128]{3,1,0,2:T(8,128)(2,1)} copy(bf16[16,256,8,128]{1,3,2,0:T(8,128)(2,1)} %get-tuple-element.28) | data formatting | bytes 16777216
  364.6 12.3 %fusion = f32[256,8,128,1]{0,2,3,1:T(8,128)S(1)} fusion(bf16[16,256,8,128]{3,1,0,2:T(8,128)(2,1)} %copy.68, bf16[16,256,8,128]{3,1,0,2:T(8,128)(2,1)} %copy.67, bf16[16,256,8,128]{3,1,0,2:T(8,128)(2,1)} %copy.66, bf16[16,384,128]{1,2,0:T(8,128)(2,1)S(1)} %copy.55), kind=kOutput, calls=%fused_computation | convolution fusion | flops 3296722944 | bytes 27787264 | tf_op jit(solution)/shard_map/krbp,kpq->rbq/dot_general | solution.py:102
  376.9 2.4 broadcast_multiply_fusion
  379.3 170.4 %reduce-scatter.2.cloned.1.call-done = f32[4,256,32]{1,2,0:T(8,128)} async-done(((f32[4,256,1024]{1,2,0:T(8,128)}), f32[4,256,32]{1,2,0:T(8,128)}) %reduce-scatter.2.cloned.1.call-update) | async-done | bytes 131088 | tf_op jit(solution)/shard_map/reduce_scatter | solution.py:109
  (38 shorter events, 9.7 us)
Async XLA Ops:
  7.2 4.7 copy-start
  7.2 171.5 %copy-start.6 = (s32[1,256]{1,0:T(1,128)S(1)}, s32[1,256]{1,0:T(1,128)}, u32[]{:S(2)}) copy-start(s32[1,256]{1,0:T(1,128)} %param.17) | copy-start | bytes 3076
  7.2 157.8 %all-gather.2.cloned.1.call-start = ((), (), s32[]{:S(2)}) async-start(), calls=%async_computation.1 | async-start | bytes 2162688 | tf_op jit(solution)/shard_map/all_gather | solution.py:74
  8.8 541.0 %reduce-scatter.2.cloned.1.call-start = ((), (), s32[]{:S(2)}) async-start(), calls=%async_computation.2 | async-start | bytes 4325376 | tf_op jit(solution)/shard_map/reduce_scatter | solution.py:109
  170.7 8.0 %collective-permute-start = (bf16[10,1024]{1,0:T(8,128)(2,1)S(1)}, bf16[10,1024]{1,0:T(8,128)(2,1)S(1)}, u32[]{:S(2)}, u32[]{:S(2)}) collective-permute-start(bf16[10,1024]{1,0:T(8,128)(2,1)S(1)} %get-tuple-element.34), channel_id=1, source_target_pairs={{0,1},{1,2},{2,3},{4,5},{5,6},{6,7},{8,9},{9,10},{10,11},{12,13},{... | collective-permute-start | bytes 61448 | tf_op jit(solution)/shard_map/ppermute | solution.py:15
  172.7 6.7 %collective-permute-start.1 = (bf16[10,1024]{1,0:T(8,128)(2,1)S(1)}, bf16[10,1024]{1,0:T(8,128)(2,1)S(1)}, u32[]{:S(2)}, u32[]{:S(2)}) collective-permute-start(bf16[10,1024]{1,0:T(8,128)(2,1)S(1)} %get-tuple-element.35), channel_id=1, source_target_pairs={{1,0},{2,1},{3,2},{5,4},{6,5},{7,6},{9,8},{10,9},{11,10},{13,12},{... | collective-permute-start | bytes 61448 | tf_op jit(solution)/shard_map/ppermute | solution.py:17
  182.9 1.4 copy-start.3
  213.8 13.0 %copy-start.5 = (bf16[1,256,1024]{2,1,0:T(8,128)(2,1)S(1)}, bf16[1,256,1024]{2,1,0:T(8,128)(2,1)}, u32[]{:S(2)}) copy-start(bf16[1,256,1024]{2,1,0:T(8,128)(2,1)} %param.15) | copy-start | bytes 1572868
  227.0 17.7 %copy-start.2 = (f32[1,256,1024]{2,1,0:T(8,128)}, f32[1,256,1024]{2,1,0:T(8,128)S(1)}, u32[]{:S(2)}) copy-start(f32[1,256,1024]{2,1,0:T(8,128)S(1)} %fusion.31) | copy-start | bytes 3145732
  227.0 22.0 %copy-start.4 = (s32[384,128]{1,0:T(8,128)S(1)}, s32[384,128]{1,0:T(8,128)}, u32[]{:S(2)}) copy-start(s32[384,128]{1,0:T(8,128)} %subtract_add_fusion) | copy-start | bytes 589828
  247.1 22.6 %collective-permute-start.2 = (bf16[16,10,1024]{2,1,0:T(8,128)(2,1)}, bf16[16,10,1024]{2,1,0:T(8,128)(2,1)}, u32[]{:S(2)}, u32[]{:S(2)}) collective-permute-start(bf16[16,10,1024]{2,1,0:T(8,128)(2,1)} %get-tuple-element.30), channel_id=1, source_target_pairs={{0,1},{1,2},{2,3},{4,5},{5,6},{6,7},{8,9},{9,10},{10,11},{12,13},{... | collective-permute-start | bytes 983048 | tf_op jit(solution)/shard_map/ppermute | solution.py:27
  250.1 27.1 %collective-permute-start.3 = (bf16[16,10,1024]{2,1,0:T(8,128)(2,1)}, bf16[16,10,1024]{2,1,0:T(8,128)(2,1)}, u32[]{:S(2)}, u32[]{:S(2)}) collective-permute-start(bf16[16,10,1024]{2,1,0:T(8,128)(2,1)} %get-tuple-element.29), channel_id=1, source_target_pairs={{1,0},{2,1},{3,2},{5,4},{6,5},{7,6},{9,8},{10,9},{11,10},{13,12},{... | collective-permute-start | bytes 983048 | tf_op jit(solution)/shard_map/ppermute | solution.py:27
  376.9 172.8 %copy-start.1 = (bf16[16,21]{1,0:T(8,128)(2,1)S(1)}, bf16[16,21]{1,0:T(8,128)(2,1)}, u32[]{:S(2)}) copy-start(bf16[16,21]{1,0:T(8,128)(2,1)} %param.12) | copy-start | bytes 2020
Sparse Core Ops, SparseCore 0:
  10.2 154.7 all-gather.1
  379.4 170.2 reduce-scatter.1
where the time goes:
time: 559 us; the launch traced here: 557 us
  waiting for transfers between devices  320 us (57%)
  local copies, waits for them, and re-layouts  132 us (24%)
  matrix products  55.8 us (10%)
  other arithmetic  18.3 us (3%)
  between operations  15.9 us (3%)
  starting transfers between devices  14.4 us (3%)
    reduce_scatter x1, waiting for transfers between devices, body(): lax.psum_scatter(selector[:, None, None] * own_term[None], 'exp', scatter...  170 us
    all_gather x1, waiting for transfers between devices, body(): all_cells = lax.all_gather(latent, 'exp', axis=2, tiled=True)  149 us
    unnamed x23, local copies, waits for them, and re-layouts  51.4 us
    convert_element_type x2, local copies, waits for them, and re-layouts, body(): rowblur.reshape(kernel_count, strip_rows + 2 * halfwidth, cell_width)  22.3 us
    dot_general x1, matrix products, body(): jnp.einsum('kyi,kyx->kix', matrix, weighted, preferred_element_type=jnp.f...  17.7 us
    slice x2, local copies, waits for them, and re-layouts, stacked_blocks(): blocked[..., :-2, :]  17 us
    dot_general x1, matrix products, body(): jnp.einsum('kyi,kix->kyx', matrix, rowblur, preferred_element_type=jnp.fl...  13 us
    slice x1, local copies, waits for them, and re-layouts, body(): middle = colback_ext[:, halfwidth:strip_rows + halfwidth]  12.6 us
  transfers between devices with their start and end apart: 6, of which 3 were waited for; matrix products, arithmetic and copies ran while one was open for 5% of the time, Pallas kernels for 0%

commit v1 on v0

--- a/solution.py
+++ b/solution.py
@@ -71,7 +71,9 @@
     position = lax.axis_index("exp")
     cell_list = cell_of[:, 0]
     own_cell = lax.dynamic_index_in_dim(cell_list, position, 0, keepdims=False)
-    all_cells = lax.all_gather(latent, "exp", axis=2, tiled=True)
+    all_cells = jnp.concatenate(
+        lax.all_to_all(jnp.stack([latent] * lax.axis_size("exp")), "exp", 0, 0), axis=2
+    )
     cell_strip = lax.dynamic_index_in_dim(all_cells, own_cell, 0, keepdims=False)
     extended = padded_2(cell_strip, (("row", 0),), halfwidth)
     rowblur = jnp.einsum(

time: 559 us -> 441 us (0.79)
  waiting for transfers between devices: 320 us -> 195 us
  starting transfers between devices: 14.4 us -> 23.6 us
    all_gather x1 -> x0, waiting for transfers between devices: 149 us -> none  [body(): all_cells = lax.all_gather(latent, 'exp', axis=2, tiled=True)]
    all_to_all x0 -> x1, waiting for transfers between devices: none -> 22.6 us  [body(): lax.all_to_all(jnp.stack([latent] * lax.axis_size('exp')), 'exp', 0, 0)]
    all_to_all x0 -> x1, starting transfers between devices: none -> 9.1 us  [body(): lax.all_to_all(jnp.stack([latent] * lax.axis_size('exp')), 'exp', 0, 0)]
    unnamed x23 -> x25, local copies, waits for them, and re-layouts: 51.4 us -> 47.6 us
  transfers between devices with their start and end apart: 6 -> 6, of which waited for: 3 -> 4; matrix products, arithmetic and copies ran while one was open for 5% -> 7% of each run, Pallas kernels for 0% -> 0%
where the time goes in v1:
time: 441 us; the launch traced here: 439 us
  waiting for transfers between devices  195 us (44%)
  local copies, waits for them, and re-layouts  132 us (30%)
  matrix products  55.2 us (13%)
  starting transfers between devices  23.6 us (5%)
  other arithmetic  17.4 us (4%)
  between operations  16.3 us (4%)
    reduce_scatter x1, waiting for transfers between devices, body(): lax.psum_scatter(selector[:, None, None] * own_term[None], 'exp', scatter...  169 us
    unnamed x25, local copies, waits for them, and re-layouts  47.6 us
    all_to_all x1, waiting for transfers between devices, body(): lax.all_to_all(jnp.stack([latent] * lax.axis_size('exp')), 'exp', 0, 0)  22.6 us
    convert_element_type x2, local copies, waits for them, and re-layouts, body(): rowblur.reshape(kernel_count, strip_rows + 2 * halfwidth, cell_width)  22.3 us
    dot_general x1, matrix products, body(): jnp.einsum('kyi,kyx->kix', matrix, weighted, preferred_element_type=jnp.f...  17.7 us
    slice x2, local copies, waits for them, and re-layouts, stacked_blocks(): blocked[..., :-2, :]  17 us
    dot_general x1, matrix products, body(): jnp.einsum('kyi,kix->kyx', matrix, rowblur, preferred_element_type=jnp.fl...  13 us
    slice x1, local copies, waits for them, and re-layouts, body(): middle = colback_ext[:, halfwidth:strip_rows + halfwidth]  12.6 us
  transfers between devices with their start and end apart: 6, of which 4 were waited for; matrix products, arithmetic and copies ran while one was open for 7% of the time, Pallas kernels for 0%

profile of v1, /device:TPU:4, one launch (start us, length us, event | category | flops | bytes accessed | tf_op | source)
XLA Modules:
  0.0 438.9 jit_solution(11858010761935252944)
XLA Ops:
  7.2 2.4 stack.2
  9.6 9.1 %all-to-all-start = ((bf16[32,4,256,32]{2,3,1,0:T(8,128)(2,1)}), bf16[32,4,256,32]{2,3,1,0:T(8,128)(2,1)}, u32[]{:S(2)}, u32[]{:S(2)}) async-start(bf16[32,4,256,32]{2,3,1,0:T(8,128)(2,1)} %stack.2), calls=%async_computation | async-start | bytes 4194304 | tf_op jit(solution)/shard_map/all_to_all | solution.py:75
  22.3 2.3 fusion.28
  24.6 1.5 convert_bitcast_fusion.1
  26.1 22.6 %all-to-all-done = bf16[32,4,256,32]{2,3,1,0:T(8,128)(2,1)} async-done(((bf16[32,4,256,32]{2,3,1,0:T(8,128)(2,1)}), bf16[32,4,256,32]{2,3,1,0:T(8,128)(2,1)}, u32[]{:S(2)}, u32[]{:S(2)}) %all-to-all-start) | async-done | bytes 2097184 | tf_op jit(solution)/shard_map/all_to_all | solution.py:75
  48.7 1.8 copy.44
  51.3 1.9 collective-permute-start
  53.2 5.3 %collective-permute-start.1 = (bf16[10,1024]{0,1:T(8,128)(2,1)}, bf16[10,1024]{0,1:T(8,128)(2,1)}, u32[]{:S(2)}, u32[]{:S(2)}) collective-permute-start(bf16[10,1024]{0,1:T(8,128)(2,1)} %get-tuple-element.32), channel_id=1, source_target_pairs={{1,0},{2,1},{3,2},{5,4},{6,5},{7,6},{9,8},{10,9},{11,10},{13,12},{... | collective-permute-start | bytes 61448 | tf_op jit(solution)/shard_map/ppermute | solution.py:17
  58.8 2.0 collective-permute-done
  67.6 7.2 %convert_bitcast_fusion = bf16[16,276,8,128]{3,1,2,0:T(8,128)(2,1)} fusion(bf16[276,8,128]{2,0,1:T(8,128)(2,1)S(1)} %copy.69, bf16[276,8,128]{2,0,1:T(8,128)(2,1)S(1)} %copy.68, bf16[276,8,128]{2,0,1:T(8,128)(2,1)S(1)} %copy.67, bf16[16,384,128,1]{2,0,1,3:T(8,128)(2,1)S(1)} %copy-done.3), kind=kOutput, calls=%fused_computation.10 | convolution fusion | flops 3482492928 | bytes 12312576 | tf_op jit(solution)/shard_map/rbp,kpq->krbq/dot_general | solution.py:79
  74.8 8.3 %copy.65 = bf16[16,276,8,128]{3,2,1,0:T(8,128)(2,1)} copy(bf16[16,276,8,128]{3,1,2,0:T(8,128)(2,1)} %convert_bitcast_fusion) | data formatting | bytes 18087936 | tf_op jit(solution)/shard_map/convert_element_type | solution.py:85
  83.1 14.0 %reshape.153 = bf16[16,276,1024]{2,1,0:T(8,128)(2,1)} reshape(bf16[16,276,8,128]{3,2,1,0:T(8,128)(2,1)} %copy.65) | data formatting | bytes 18087936 | tf_op jit(solution)/shard_map/convert_element_type | solution.py:85
  97.1 13.0 %fusion.6 = f32[256,1024]{1,0:T(8,128)S(1)} fusion(bf16[16,276,1024]{2,1,0:T(8,128)(2,1)} %reshape.153, bf16[1,16,256,1024]{3,2,1,0:T(8,128)(2,1)} %param.14, bf16[16,256,276]{1,0,2:T(8,128)(2,1)S(1)} %convert_bitcast_fusion.1), kind=kOutput, calls=%fused_computation.8 | convolution fusion | flops 2327576576 | bytes 20742144 | tf_op jit(solution)/shard_map/kyi,kix->kyx/dot_general | solution.py:89
  110.3 17.7 %fusion.45 = (bf16[16,276,1024]{2,1,0:T(8,128)(2,1)}, f32[16,276,1024]{2,1,0:T(8,128)}) fusion(bf16[1,16,256,1024]{3,2,1,0:T(8,128)(2,1)} %param.14, f32[256,1024]{1,0:T(8,128)S(1)} %bitcast.59, bf16[16,256,276]{1,0,2:T(8,128)(2,1)S(1)} %convert_bitcast_fusion.1), kind=kOutput, calls=%fused_computation.67 | convolution fusion | flops 2332360704 | bytes 38830080 | tf_op jit(solution)/shard_map/kyi,kyx->kix/dot_general | solution.py:95
  128.0 2.4 fusion.43
  130.3 1.9 collective-permute-start.2
  133.4 5.3 %collective-permute-start.3 = (bf16[16,10,1024]{2,1,0:T(8,128)(2,1)}, bf16[16,10,1024]{2,1,0:T(8,128)(2,1)}, u32[]{:S(2)}, u32[]{:S(2)}) collective-permute-start(bf16[16,10,1024]{2,1,0:T(8,128)(2,1)} %get-tuple-element.29), channel_id=1, source_target_pairs={{1,0},{2,1},{3,2},{5,4},{6,5},{7,6},{9,8},{10,9},{11,10},{13,12},{... | collective-permute-start | bytes 983048 | tf_op jit(solution)/shard_map/ppermute | solution.py:27
  140.6 12.6 %slice.108 = f32[16,256,1024]{2,1,0:T(8,128)} slice(f32[16,276,1024]{2,1,0:T(8,128)} %get-tuple-element.37), slice={[0:16], [10:266], [0:1024]} | slice | bytes 33554432 | tf_op jit(solution)/shard_map/slice | solution.py:100
  153.2 1.7 slice_add_fusion.1
  154.9 5.8 %scatter-add.6 = f32[16,256,1024]{2,1,0:T(8,128)} dynamic-update-slice(f32[16,256,1024]{2,1,0:T(8,128)} %slice.108, f32[16,10,1024]{2,1,0:T(8,128)S(1)} %slice_add_fusion.1, s32[]{:T(128)} %constant.75.clone.1, s32[]{:T(128)} %constant.75.clone.1, s32[]{:T(128)} %constant.75.clone.1) | dynamic-update-slice | bytes 1310724 | tf_op jit(solution)/shard_map/scatter-add | solution.py:101
  160.8 1.5 slice_add_fusion
  162.3 5.1 %scatter-add.9 = f32[16,256,1024]{2,1,0:T(8,128)} dynamic-update-slice(f32[16,256,1024]{2,1,0:T(8,128)} %scatter-add.6, f32[16,10,1024]{2,1,0:T(8,128)S(1)} %slice_add_fusion, s32[]{:T(128)} %constant.75.clone.1, s32[]{:T(128)} %constant.82.clone.1, s32[]{:T(128)} %constant.75.clone.1) | dynamic-update-slice | bytes 1310724 | tf_op jit(solution)/shard_map/scatter-add | solution.py:102
  167.4 9.1 %convert_element_type.94 = bf16[16,256,1024]{2,1,0:T(8,128)(2,1)} convert(f32[16,256,1024]{2,1,0:T(8,128)} %scatter-add.9) | non-fusion elementwise | flops 4194304 | bytes 25165824 | tf_op jit(solution)/shard_map/convert_element_type | solution.py:103
  176.5 12.3 %copy.73 = bf16[16,256,1024]{1,2,0:T(8,128)(2,1)} copy(bf16[16,256,1024]{2,1,0:T(8,128)(2,1)} %convert_element_type.94) | data formatting | bytes 16777216
  188.8 8.4 %pad.13.clone = bf16[16,256,1280]{1,2,0:T(8,128)(2,1)} pad(bf16[16,256,1024]{1,2,0:T(8,128)(2,1)} %copy.73, bf16[]{:T(256)} %constant.80.clone.1), padding=0_0x0_0x128_128 | pad | bytes 18874370 | tf_op jit(solution)/shard_map/jit(_pad)/pad | solution.py:57
  197.2 16.7 %fusion.42 = (bf16[16,256,8,128]{1,3,2,0:T(8,128)(2,1)}, bf16[16,256,8,128]{1,3,2,0:T(8,128)(2,1)}, bf16[16,256,8,128]{1,3,2,0:T(8,128)(2,1)}) fusion(bf16[16,256,10,128]{1,3,2,0:T(8,128)(2,1)} %bitcast.56), kind=kLoop, calls=%fused_computation.64 | loop fusion | bytes 50331648 | tf_op jit(solution)/shard_map/slice | solution.py:60
  213.9 11.4 %copy.70 = bf16[16,256,8,128]{3,1,0,2:T(8,128)(2,1)} copy(bf16[16,256,8,128]{1,3,2,0:T(8,128)(2,1)} %get-tuple-element.26) | data formatting | bytes 16777216
  225.3 11.4 %copy.71 = bf16[16,256,8,128]{3,1,0,2:T(8,128)(2,1)} copy(bf16[16,256,8,128]{1,3,2,0:T(8,128)(2,1)} %get-tuple-element.27) | data formatting | bytes 16777216
  236.7 11.4 %copy.72 = bf16[16,256,8,128]{3,1,0,2:T(8,128)(2,1)} copy(bf16[16,256,8,128]{1,3,2,0:T(8,128)(2,1)} %get-tuple-element.28) | data formatting | bytes 16777216
  248.1 12.3 %fusion = f32[256,8,128,1]{0,2,3,1:T(8,128)S(1)} fusion(bf16[16,256,8,128]{3,1,0,2:T(8,128)(2,1)} %copy.72, bf16[16,256,8,128]{3,1,0,2:T(8,128)(2,1)} %copy.71, bf16[16,256,8,128]{3,1,0,2:T(8,128)(2,1)} %copy.70, bf16[16,384,128]{1,2,0:T(8,128)(2,1)S(1)} %copy.60), kind=kOutput, calls=%fused_computation | convolution fusion | flops 3296722944 | bytes 27787264 | tf_op jit(solution)/shard_map/krbp,kpq->rbq/dot_general | solution.py:104
  260.4 2.4 broadcast_multiply_fusion
  262.8 169.3 %reduce-scatter.2.cloned.1.call-done = f32[4,256,32]{1,2,0:T(8,128)} async-done(((f32[4,256,1024]{1,2,0:T(8,128)}), f32[4,256,32]{1,2,0:T(8,128)}) %reduce-scatter.2.cloned.1.call-update) | async-done | bytes 131088 | tf_op jit(solution)/shard_map/reduce_scatter | solution.py:111
  (44 shorter events, 12.6 us)
Async XLA Ops:
  7.2 15.1 %copy-start = (bf16[16,21]{1,0:T(8,128)(2,1)S(1)}, bf16[16,21]{1,0:T(8,128)(2,1)}, u32[]{:S(2)}) copy-start(bf16[16,21]{1,0:T(8,128)(2,1)} %param.12) | copy-start | bytes 2020
  7.2 11.6 %copy-start.8 = (s32[32,1]{0,1:T(1,128)S(1)}, s32[32,1]{0,1:T(1,128)}, u32[]{:S(2)}) copy-start(s32[32,1]{0,1:T(1,128)} %param.16) | copy-start | bytes 388
  7.2 13.5 %copy-start.7 = (s32[1,256]{1,0:T(1,128)S(1)}, s32[1,256]{1,0:T(1,128)}, u32[]{:S(2)}) copy-start(s32[1,256]{1,0:T(1,128)} %param.17) | copy-start | bytes 3076
  7.2 17.4 %copy-start.6 = (bf16[16,21]{1,0:T(8,128)(2,1)S(1)}, bf16[16,21]{1,0:T(8,128)(2,1)}, u32[]{:S(2)}) copy-start(bf16[16,21]{1,0:T(8,128)(2,1)} %param.13) | copy-start | bytes 2020
  9.6 39.0 %all-to-all-start = ((bf16[32,4,256,32]{2,3,1,0:T(8,128)(2,1)}), bf16[32,4,256,32]{2,3,1,0:T(8,128)(2,1)}, u32[]{:S(2)}, u32[]{:S(2)}) async-start(bf16[32,4,256,32]{2,3,1,0:T(8,128)(2,1)} %stack.2), calls=%async_computation | async-start | bytes 4194304 | tf_op jit(solution)/shard_map/all_to_all | solution.py:75
  18.8 413.3 %reduce-scatter.2.cloned.1.call-start = ((), (), s32[]{:S(2)}) async-start(), calls=%async_computation.2 | async-start | bytes 4325376 | tf_op jit(solution)/shard_map/reduce_scatter | solution.py:111
  51.3 9.5 %collective-permute-start = (bf16[10,1024]{0,1:T(8,128)(2,1)}, bf16[10,1024]{0,1:T(8,128)(2,1)}, u32[]{:S(2)}, u32[]{:S(2)}) collective-permute-start(bf16[10,1024]{0,1:T(8,128)(2,1)} %get-tuple-element.31), channel_id=1, source_target_pairs={{0,1},{1,2},{2,3},{4,5},{5,6},{6,7},{8,9},{9,10},{10,11},{12,13},{... | collective-permute-start | bytes 61448 | tf_op jit(solution)/shard_map/ppermute | solution.py:15
  53.2 9.3 %collective-permute-start.1 = (bf16[10,1024]{0,1:T(8,128)(2,1)}, bf16[10,1024]{0,1:T(8,128)(2,1)}, u32[]{:S(2)}, u32[]{:S(2)}) collective-permute-start(bf16[10,1024]{0,1:T(8,128)(2,1)} %get-tuple-element.32), channel_id=1, source_target_pairs={{1,0},{2,1},{3,2},{5,4},{6,5},{7,6},{9,8},{10,9},{11,10},{13,12},{... | collective-permute-start | bytes 61448 | tf_op jit(solution)/shard_map/ppermute | solution.py:17
  66.2 1.4 copy-start.3
  97.1 13.0 %copy-start.5 = (bf16[1,256,1024]{2,1,0:T(8,128)(2,1)S(1)}, bf16[1,256,1024]{2,1,0:T(8,128)(2,1)}, u32[]{:S(2)}) copy-start(bf16[1,256,1024]{2,1,0:T(8,128)(2,1)} %param.15) | copy-start | bytes 1572868
  110.3 17.7 %copy-start.2 = (f32[1,256,1024]{2,1,0:T(8,128)}, f32[1,256,1024]{2,1,0:T(8,128)S(1)}, u32[]{:S(2)}) copy-start(f32[1,256,1024]{2,1,0:T(8,128)S(1)} %fusion.31) | copy-start | bytes 3145732
  110.3 22.0 %copy-start.4 = (s32[384,128]{1,0:T(8,128)S(1)}, s32[384,128]{1,0:T(8,128)}, u32[]{:S(2)}) copy-start(s32[384,128]{1,0:T(8,128)} %subtract_add_fusion) | copy-start | bytes 589828
  130.3 22.9 %collective-permute-start.2 = (bf16[16,10,1024]{2,1,0:T(8,128)(2,1)}, bf16[16,10,1024]{2,1,0:T(8,128)(2,1)}, u32[]{:S(2)}, u32[]{:S(2)}) collective-permute-start(bf16[16,10,1024]{2,1,0:T(8,128)(2,1)} %get-tuple-element.30), channel_id=1, source_target_pairs={{0,1},{1,2},{2,3},{4,5},{5,6},{6,7},{8,9},{9,10},{10,11},{12,13},{... | collective-permute-start | bytes 983048 | tf_op jit(solution)/shard_map/ppermute | solution.py:27
  133.4 27.4 %collective-permute-start.3 = (bf16[16,10,1024]{2,1,0:T(8,128)(2,1)}, bf16[16,10,1024]{2,1,0:T(8,128)(2,1)}, u32[]{:S(2)}, u32[]{:S(2)}) collective-permute-start(bf16[16,10,1024]{2,1,0:T(8,128)(2,1)} %get-tuple-element.29), channel_id=1, source_target_pairs={{1,0},{2,1},{3,2},{5,4},{6,5},{7,6},{9,8},{10,9},{11,10},{13,12},{... | collective-permute-start | bytes 983048 | tf_op jit(solution)/shard_map/ppermute | solution.py:27
  260.4 171.7 %copy-start.1 = (bf16[16,21]{1,0:T(8,128)(2,1)S(1)}, bf16[16,21]{1,0:T(8,128)(2,1)}, u32[]{:S(2)}) copy-start(bf16[16,21]{1,0:T(8,128)(2,1)} %param.12) | copy-start | bytes 2020
Sparse Core Ops, SparseCore 0:
  262.9 169.1 reduce-scatter.1
